TPU v7x, 32 devices: a whole 2x2x4 slice. The times are simulated.
32 devices in a mesh: dp: 16 (over z, y, core), mp: 2 (over x).
Axes of the slice: x: 2, y: 2, z: 4, core: 2. Of those that a mesh axis runs over, the one named last changes fastest.
Arguments:
- layer_input: bfloat16 [2, 16, 256, 2048], P(None, 'dp', 'mp')
- out_grad: bfloat16 [2, 16, 256, 2048], P(None, 'dp', 'mp')
- valid_count: int32 [2, 16], P(None, 'dp'), may hold values from 129 to 256, as said below
- w_query: bfloat16 [2048, 2048], P('dp', 'mp'), may hold values from -0.125 to 0.125
- w_key: bfloat16 [2048, 2048], P('dp', 'mp'), may hold values from -0.125 to 0.125
- w_value: bfloat16 [2048, 2048], P('dp', 'mp'), may hold values from -0.125 to 0.125
- w_output: bfloat16 [2048, 2048], P('dp', 'mp'), may hold values from -0.75 to 0.75
- w_gate: bfloat16 [2048, 8192], P('dp', 'mp'), may hold values from -0.125 to 0.125
- w_up: bfloat16 [2048, 8192], P('dp', 'mp'), may hold values from -0.125 to 0.125
- w_down: bfloat16 [2048, 8192], P('dp', 'mp'), may hold values from -0.0625 to 0.0625
- gain_attn: float32 [2048], replicated, may hold values from 0.5 to 1.5
- gain_mlp: float32 [2048], replicated, may hold values from 0.5 to 1.5
- memory_gate: float32 [16], replicated, may hold values from -3 to 3
Outputs:
- layer_output: bfloat16 [2, 16, 256, 2048], P(None, 'dp', 'mp')
- grad_input: float32 [2, 16, 256, 2048], P(None, 'dp', 'mp')
- grad_query: float32 [2048, 2048], P('dp', 'mp')
- grad_key: float32 [2048, 2048], P('dp', 'mp')
- grad_value: float32 [2048, 2048], P('dp', 'mp')
- grad_output: float32 [2048, 2048], P('dp', 'mp')
- grad_gate: float32 [2048, 8192], P('dp', 'mp')
- grad_up: float32 [2048, 8192], P('dp', 'mp')
- grad_down: float32 [2048, 8192], P('dp', 'mp')
- grad_norm_attn: float32 [2048], replicated
- grad_norm_mlp: float32 [2048], replicated
- grad_memory_gate: float32 [16], replicated
Inputs may be any that keep to these rules, and one draw needn't show every extreme that they name: valid_count counts the valid leading tokens of each sequence; its first segment is always full and some sequence is full to 256.
All inputs are finite; a program needn't handle non-finite values.
Results may differ from a plain program's by a relative error of at most 0.014.
Values may be sent and summed in bfloat16 or wider, within the bound.
No kernel may reach another device: no remote copies, remote signals or barrier semaphores. Data moves between devices by JAX's collectives and lax.ppermute only.
A program may use at most 448 MiB of HBM per device.

v0:
```python
import jax
import jax.numpy as jnp
from jax import lax
from jax.sharding import PartitionSpec as P

HD = 128
epsilon = 1e-05
masked_score = -1e30


def positive_map(values):
    return jnp.where(values > 0.0, values + 1.0, jnp.exp(jnp.minimum(values, 0.0)))


def positive_slope(values):
    return jnp.where(values > 0.0, 1.0, jnp.exp(jnp.minimum(values, 0.0)))


def gather_rows(local_rows):
    return lax.all_gather(local_rows, "mp", axis=1, tiled=True)


def reduce_rows(partial_value):
    return lax.psum_scatter(partial_value, "mp", scatter_dimension=1, tiled=True)


def fold_weights(inputs, weight):
    return jnp.dot(inputs, weight, preferred_element_type=jnp.float32)


def map_weights(inputs, weight):
    return lax.dot_general(
        inputs, weight, (((1,), (1,)), ((), ())), preferred_element_type=jnp.float32
    )


def make_term(pairs_list):
    columns = []
    for index in range(4):
        total = None
        for pairs in pairs_list:
            left_part = pairs[index][0]
            addend = lax.dot_general(
                left_part,
                pairs[index][1],
                (((0,), (0,)), ((), ())),
                preferred_element_type=jnp.float32,
            )
            total = addend if total is None else total + addend
        columns.append(total)
    return jnp.concatenate(columns, axis=1)


def run_block(
    local_in, local_grad, counts, w_qkv, w_output, w_gu, w_down, gain_attn, gain_mlp, gate_local
):
    seq_count, rows_local, width = local_in.shape
    full_len = rows_local * lax.axis_size("mp")
    seg_len = full_len // 2
    heads_local = gate_local.shape[0]
    attn_width = heads_local * HD
    ff_width = w_down.shape[1]
    total_rows = seq_count * full_len
    score_scale = HD ** (-0.5)
    shape_heads = (seq_count, 2, seg_len, heads_local, HD)
    valid_rows = (jnp.arange(full_len)[None, :] < counts[:, None]).astype(jnp.float32)
    inputs = local_in.astype(jnp.float32)
    inv_first = lax.rsqrt(jnp.mean(inputs * inputs, axis=-1, keepdims=True) + epsilon)
    normed = (inputs * inv_first * gain_attn).astype(jnp.bfloat16)
    normed_all = gather_rows(normed).reshape(total_rows, width)
    qkv_rows = fold_weights(normed_all, w_qkv).astype(jnp.bfloat16)
    queries = qkv_rows[:, :attn_width].reshape(shape_heads)
    key_rows = qkv_rows[:, attn_width : 2 * attn_width].reshape(shape_heads)
    value_rows = qkv_rows[:, 2 * attn_width :].reshape(shape_heads)
    raw_scores = (
        jnp.einsum("bnqhe,bnkhe->bnhqk", queries, key_rows, preferred_element_type=jnp.float32)
        * score_scale
    )
    seg_pos = jnp.arange(seg_len)
    causal = seg_pos[:, None] >= seg_pos[None, :]
    key_valid = valid_rows.reshape(seq_count, 2, 1, 1, seg_len) > 0.5
    scores = jnp.where(causal & key_valid, raw_scores, masked_score)
    top_score = jnp.max(scores, axis=-1, keepdims=True)
    exponent = jnp.exp(scores - top_score)
    probability = exponent / jnp.sum(exponent, axis=-1, keepdims=True)
    prob_low = probability.astype(jnp.bfloat16)
    local_out = jnp.einsum(
        "bnhqk,bnkhe->bnqhe", prob_low, value_rows, preferred_element_type=jnp.float32
    )
    query_map = positive_map(queries[:, 1].astype(jnp.float32)).astype(jnp.bfloat16)
    seg_valid = valid_rows[:, :seg_len].reshape(seq_count, seg_len, 1, 1)
    key_map = (
        positive_map(key_rows[:, 0].astype(jnp.float32)).astype(jnp.bfloat16).astype(jnp.float32)
        * seg_valid
    )
    key_map_low = key_map.astype(jnp.bfloat16)
    memory = jnp.einsum(
        "bthe,bthf->bhef", key_map_low, value_rows[:, 0], preferred_element_type=jnp.float32
    )
    memory_low = memory.astype(jnp.bfloat16)
    normalizer = jnp.sum(key_map, axis=1)
    numerator = jnp.einsum(
        "bthe,bhef->bthf", query_map, memory_low, preferred_element_type=jnp.float32
    )
    denominator = jnp.sum(query_map.astype(jnp.float32) * normalizer[:, None], axis=-1)
    retrieved = numerator / denominator[..., None]
    gate_sig = jax.nn.sigmoid(gate_local)
    gate_value = gate_sig[:, None]
    first_seg = (1.0 - gate_value) * local_out[:, 0]
    second = gate_value * retrieved + (1.0 - gate_value) * local_out[:, 1]
    combined = jnp.stack([first_seg, second], axis=1).reshape(seq_count, full_len, attn_width)
    heads_out = (
        (combined * valid_rows[..., None]).astype(jnp.bfloat16).reshape(total_rows, attn_width)
    )
    attn_out = reduce_rows(map_weights(heads_out, w_output).reshape(seq_count, full_len, width))
    hidden_state = inputs + attn_out
    inv_second = lax.rsqrt(jnp.mean(hidden_state * hidden_state, axis=-1, keepdims=True) + epsilon)
    normed_mlp = (hidden_state * inv_second * gain_mlp).astype(jnp.bfloat16)
    mlp_in = gather_rows(normed_mlp).reshape(total_rows, width)
    gate_up = fold_weights(mlp_in, w_gu)
    gate_pre = gate_up[:, :ff_width]
    up_pre = gate_up[:, ff_width:]
    sigma = jax.nn.sigmoid(gate_pre)
    activated = (gate_pre * sigma * up_pre).astype(jnp.bfloat16)
    mlp_out = reduce_rows(map_weights(activated, w_down).reshape(seq_count, full_len, width))
    layer_out = (hidden_state + mlp_out).astype(jnp.bfloat16)
    grad_rows = gather_rows(local_grad).reshape(total_rows, width)
    act_back = fold_weights(grad_rows, w_down)
    gate_back = (act_back * up_pre * sigma * (1.0 + gate_pre * (1.0 - sigma))).astype(jnp.bfloat16)
    up_back = (act_back * gate_pre * sigma).astype(jnp.bfloat16)
    grad_gu = jnp.concatenate([gate_back, up_back], axis=1)
    mlp_back = reduce_rows(map_weights(grad_gu, w_gu).reshape(seq_count, full_len, width))
    scaled_mlp = mlp_back * gain_mlp
    hidden_back = local_grad.astype(jnp.float32) + inv_second * (
        scaled_mlp
        - hidden_state
        * inv_second
        * inv_second
        * jnp.mean(scaled_mlp * hidden_state, axis=-1, keepdims=True)
    )
    gain_mlp_part = jnp.sum(mlp_back * hidden_state * inv_second, axis=(0, 1))
    hidden_rows = gather_rows(hidden_back.astype(jnp.bfloat16)).reshape(total_rows, width)
    heads_grad = fold_weights(hidden_rows, w_output)
    grad_comb = (
        heads_grad.reshape(seq_count, full_len, attn_width) * valid_rows[..., None]
    ).reshape(shape_heads)
    gate_sum = jnp.sum(
        grad_comb[:, 0] * -local_out[:, 0] + grad_comb[:, 1] * (retrieved - local_out[:, 1]),
        axis=(0, 1, 3),
    )
    gate_part = gate_sum * gate_sig * (1.0 - gate_sig)
    local_back = ((1.0 - gate_value) * grad_comb).astype(jnp.bfloat16)
    retrieved_back = gate_value * grad_comb[:, 1]
    numer_back = (retrieved_back / denominator[..., None]).astype(jnp.bfloat16)
    denom_back = -jnp.sum(retrieved_back * numerator, axis=-1) / (denominator * denominator)
    prob_back = jnp.einsum(
        "bnqhe,bnkhe->bnhqk", local_back, value_rows, preferred_element_type=jnp.float32
    )
    value_back = jnp.einsum(
        "bnhqk,bnqhe->bnkhe", prob_low, local_back, preferred_element_type=jnp.float32
    )
    score_back = (
        probability * (prob_back - jnp.sum(prob_back * probability, axis=-1, keepdims=True))
    ).astype(jnp.bfloat16)
    query_back = (
        jnp.einsum("bnhqk,bnkhe->bnqhe", score_back, key_rows, preferred_element_type=jnp.float32)
        * score_scale
    )
    key_back = (
        jnp.einsum("bnhqk,bnqhe->bnkhe", score_back, queries, preferred_element_type=jnp.float32)
        * score_scale
    )
    memory_back = jnp.einsum(
        "bthe,bthf->bhef", query_map, numer_back, preferred_element_type=jnp.float32
    ).astype(jnp.bfloat16)
    qmap_back = (
        jnp.einsum("bthf,bhef->bthe", numer_back, memory_low, preferred_element_type=jnp.float32)
        + denom_back[..., None] * normalizer[:, None]
    )
    norm_back = jnp.sum(denom_back[..., None] * query_map.astype(jnp.float32), axis=1)
    kmap_back = (
        jnp.einsum(
            "bthf,bhef->bthe", value_rows[:, 0], memory_back, preferred_element_type=jnp.float32
        )
        + norm_back[:, None]
    ) * seg_valid
    value_from_memory = jnp.einsum(
        "bthe,bhef->bthf", key_map_low, memory_back, preferred_element_type=jnp.float32
    )
    query_back = query_back.at[:, 1].add(
        qmap_back * positive_slope(queries[:, 1].astype(jnp.float32))
    )
    key_back = key_back.at[:, 0].add(kmap_back * positive_slope(key_rows[:, 0].astype(jnp.float32)))
    value_back = value_back.at[:, 0].add(value_from_memory)
    grad_qkv = jnp.concatenate(
        [
            query_back.reshape(total_rows, attn_width).astype(jnp.bfloat16),
            key_back.reshape(total_rows, attn_width).astype(jnp.bfloat16),
            value_back.reshape(total_rows, attn_width).astype(jnp.bfloat16),
        ],
        axis=1,
    )
    attn_back = reduce_rows(map_weights(grad_qkv, w_qkv).reshape(seq_count, full_len, width))
    scaled_attn = attn_back * gain_attn
    grad_input = hidden_back + inv_first * (
        scaled_attn
        - inputs * inv_first * inv_first * jnp.mean(scaled_attn * inputs, axis=-1, keepdims=True)
    )
    gain_attn_part = jnp.sum(attn_back * inputs * inv_first, axis=(0, 1))
    pairs = (
        (normed_all, grad_qkv),
        (hidden_rows, heads_out),
        (mlp_in, grad_gu),
        (grad_rows, activated),
    )
    return (layer_out, grad_input, pairs, gain_attn_part, gain_mlp_part, gate_part)


def on_device(
    layer_input,
    out_grad,
    valid_count,
    w_query,
    w_key,
    w_value,
    w_output,
    w_gate,
    w_up,
    w_down,
    gain_attn,
    gain_mlp,
    memory_gate,
):
    heads_local = w_query.shape[1] // HD
    head_start = lax.axis_index("mp") * heads_local
    gate_local = lax.dynamic_slice_in_dim(memory_gate, head_start, heads_local, 0)
    w_qkv_part = jnp.concatenate([w_query, w_key, w_value], axis=1)
    w_gu_part = jnp.concatenate([w_gate, w_up], axis=1)
    micro_count = layer_input.shape[0]
    outcomes = []
    for micro in range(micro_count):
        w_qkv, w_out_full, w_gu, w_down_full = (
            lax.all_gather(w_qkv_part, "dp", axis=0, tiled=True),
            lax.all_gather(w_output, "dp", axis=0, tiled=True),
            lax.all_gather(w_gu_part, "dp", axis=0, tiled=True),
            lax.all_gather(w_down, "dp", axis=0, tiled=True),
        )
        outcomes.append(
            run_block(
                layer_input[micro],
                out_grad[micro],
                valid_count[micro],
                w_qkv,
                w_out_full,
                w_gu,
                w_down_full,
                gain_attn,
                gain_mlp,
                gate_local,
            )
        )
    layer_output = jnp.stack([outcome[0] for outcome in outcomes], axis=0)
    grad_input = jnp.stack([outcome[1] for outcome in outcomes], axis=0)
    gain_attn_sum = outcomes[0][3]
    gain_mlp_sum = outcomes[0][4]
    gate_sum = outcomes[0][5]
    for outcome in outcomes[1:]:
        gain_attn_sum = gain_attn_sum + outcome[3]
        gain_mlp_sum = gain_mlp_sum + outcome[4]
        gate_sum = gate_sum + outcome[5]
    all_grads = lax.psum_scatter(
        make_term([outcome[2] for outcome in outcomes]), "dp", scatter_dimension=0, tiled=True
    )
    gate_full = lax.dynamic_update_slice_in_dim(
        jnp.zeros((memory_gate.shape[0],), jnp.float32), gate_sum, head_start, 0
    )
    grad_norm_attn, grad_norm_mlp, grad_memory_gate = lax.psum(
        (gain_attn_sum, gain_mlp_sum, gate_full), ("dp", "mp")
    )
    attn_width = w_query.shape[1]
    ff_width = w_gate.shape[1]
    grad_query = all_grads[:, :attn_width]
    grad_key = all_grads[:, attn_width : 2 * attn_width]
    grad_value = all_grads[:, 2 * attn_width : 3 * attn_width]
    grad_output = all_grads[:, 3 * attn_width : 4 * attn_width]
    mlp_start = 4 * attn_width
    grad_gate = all_grads[:, mlp_start : mlp_start + ff_width]
    grad_up = all_grads[:, mlp_start + ff_width : mlp_start + 2 * ff_width]
    grad_down = all_grads[:, mlp_start + 2 * ff_width :]
    return (
        layer_output,
        grad_input,
        grad_query,
        grad_key,
        grad_value,
        grad_output,
        grad_gate,
        grad_up,
        grad_down,
        grad_norm_attn,
        grad_norm_mlp,
        grad_memory_gate,
    )


def solution(mesh):
    in_specs = (
        P(None, "dp", "mp", None),
        P(None, "dp", "mp", None),
        P(None, "dp"),
        P("dp", "mp"),
        P("dp", "mp"),
        P("dp", "mp"),
        P("dp", "mp"),
        P("dp", "mp"),
        P("dp", "mp"),
        P("dp", "mp"),
        P(),
        P(),
        P(),
    )
    out_specs = (
        P(None, "dp", "mp", None),
        P(None, "dp", "mp", None),
        P("dp", "mp"),
        P("dp", "mp"),
        P("dp", "mp"),
        P("dp", "mp"),
        P("dp", "mp"),
        P("dp", "mp"),
        P("dp", "mp"),
        P(),
        P(),
        P(),
    )
    return jax.shard_map(
        on_device, mesh=mesh, in_specs=in_specs, out_specs=out_specs, check_vma=False
    )
```

profile of v0, /device:TPU:0, one launch (start us, length us, event | category | flops | bytes accessed | tf_op | source)
XLA Modules:
  0.0 2450.9 jit_solution(10534813084720500561)
XLA Ops:
  19.5 16.5 all-gather.27.cloned.1.call-done
  36.0 103.3 %all-gather.17.cloned.1.call-done = bf16[2048,3072]{1,0:T(8,128)(2,1)} async-done(((bf16[128,3072]{1,0:T(8,128)(2,1)}), bf16[2048,3072]{1,0:T(8,128)(2,1)}) %all-gather.17.cloned.1.call-update) | async-done | bytes 12582928 | tf_op jit(solution)/shard_map/all_gather | solution.py:243
  190.0 23.5 all-gather.19.cloned.1.call-done
  225.6 23.4 reduce-scatter.14.cloned.1.call-done
  249.0 34.6 %reduce-scatter.10.cloned.1.call-done = f32[1,128,2048]{2,1,0:T(8,128)} async-done(((f32[1,256,2048]{2,1,0:T(8,128)}), f32[1,128,2048]{2,1,0:T(8,128)}) %reduce-scatter.10.cloned.1.call-update) | async-done | bytes 1048592 | tf_op jit(solution)/shard_map/reduce_scatter | solution.py:24
  291.7 16.3 all-gather.21.cloned.1.call-done
  308.0 170.2 %all-gather.23.cloned.1.call-done = bf16[2048,8192]{1,0:T(8,128)(2,1)} async-done(((bf16[128,8192]{1,0:T(8,128)(2,1)}), bf16[2048,8192]{1,0:T(8,128)(2,1)}) %all-gather.23.cloned.1.call-update) | async-done | bytes 33554448 | tf_op jit(solution)/shard_map/all_gather | solution.py:245
  478.2 17.9 fusion.87
  501.6 128.5 %all-gather.25.cloned.1.call-done = bf16[2048,4096]{1,0:T(8,128)(2,1)} async-done(((bf16[128,4096]{1,0:T(8,128)(2,1)}), bf16[2048,4096]{1,0:T(8,128)(2,1)}) %all-gather.25.cloned.1.call-update) | async-done | bytes 16777232 | tf_op jit(solution)/shard_map/all_gather | solution.py:246
  630.1 13.1 multiply_convert_fusion.3
  643.3 17.2 convolution_bitcast_fusion.3
  660.6 30.1 %reduce-scatter.18.cloned.1.call-done = f32[1,128,2048]{2,1,0:T(8,128)} async-done(((f32[1,256,2048]{2,1,0:T(8,128)}), f32[1,128,2048]{2,1,0:T(8,128)}) %reduce-scatter.18.cloned.1.call-update) | async-done | bytes 1048592 | tf_op jit(solution)/shard_map/reduce_scatter | solution.py:24
  694.9 20.3 all-gather.29.cloned.1.call-done
  715.2 17.9 fusion.82
  738.0 13.1 multiply_convert_fusion.1
  751.2 17.2 convolution_bitcast_fusion.1
  768.5 12.6 convolution_bitcast_fusion.4
  781.2 19.3 reduce-scatter.22.cloned.1.call-done
  802.6 31.9 %reduce-scatter.16.cloned.1.call-done = f32[1,128,2048]{2,1,0:T(8,128)} async-done(((f32[1,256,2048]{2,1,0:T(8,128)}), f32[1,128,2048]{2,1,0:T(8,128)}) %reduce-scatter.16.cloned.1.call-update) | async-done | bytes 1048592 | tf_op jit(solution)/shard_map/reduce_scatter | solution.py:24
  839.0 20.6 all-gather.33.cloned.1.call-done
  872.3 10.0 all-gather.31.cloned.1.call-done
  939.5 9.6 convolution_bitcast_fusion.5
  949.6 15.0 fusion.77
  964.6 26.6 %fusion.2 = f32[2048,8192]{1,0:T(8,128)} fusion(bf16[256,4096]{1,0:T(8,128)(2,1)} %get-tuple-element.110, bf16[256,4096]{1,0:T(8,128)(2,1)} %get-tuple-element.109, bf16[1,256,2048]{2,1,0:T(8,128)(2,1)} %all-gather.21.cloned.1.call-done), kind=kOutput, calls=%fused_computation.27 | convolution fusion | flops 8598323200 | bytes 72351744 | tf_op jit(solution)/shard_map/dot_general | solution.py:43
  991.2 26.6 %add_bitcast_fusion = f32[2048,4096]{1,0:T(8,128)} fusion(f32[4096,2048]{0,1:T(8,128)} %fusion.77, bf16[256,4096]{1,0:T(8,128)(2,1)} %get-tuple-element.121, bf16[1,1,256,2048]{3,2,1,0:T(8,128)(2,1)} %all-gather.37.cloned.1.call-done), kind=kOutput, calls=%fused_computation.4 | convolution fusion | flops 4303355904 | bytes 70254592 | tf_op jit(solution)/shard_map/dot_general | solution.py:43
  1017.7 47.7 %convolution_add_fusion = f32[2048,8192]{1,0:T(8,128)} fusion(f32[2048,8192]{1,0:T(8,128)} %fusion.2, bf16[256,4096]{1,0:T(8,128)(2,1)} %get-tuple-element.112, bf16[256,4096]{1,0:T(8,128)(2,1)S(1)} %copy-done.39, bf16[1,256,2048]{2,1,0:T(8,128)(2,1)} %all-gather.29.cloned.1.call-done), kind=kOutput, calls=%fused_computation.3 | convolution fusion | flops 8615100416 | bytes 139460608 | tf_op jit(solution)/shard_map/dot_general | solution.py:43
  1072.7 9.5 copy.140
  1082.2 11.5 fusion.89
  1093.7 16.8 convolution_add_fusion.1
  1110.5 86.1 %pad_maximum_fusion = f32[2048,16384]{1,0:T(8,128)} fusion(f32[2048,4096]{1,0:T(8,128)} %add_bitcast_fusion, f32[2048,8192]{1,0:T(8,128)} %convolution_add_fusion, f32[2048,1024]{1,0:T(8,128)} %copy.140, f32[2048,3072]{1,0:T(8,128)} %convolution_add_fusion.1), kind=kLoop, calls=%fused_computation.2 | loop fusion | flops 100663296 | bytes 268435456 | tf_op jit(solution)/shard_map/concatenate | solution.py:51
  1200.0 39.8 %all-reduce = (f32[2048]{0:T(1024)}, f32[2048]{0:T(1024)}, f32[16]{0:T(128)}) all-reduce(f32[2048]{0:T(1024)S(1)} %add.328, f32[2048]{0:T(1024)S(1)} %add.329, f32[16]{0:T(128)S(1)} %fusion.166), channel_id=1, replica_groups=mesh['dp'=16,'mp'=2] {'dp','mp'}, use_global_device_ids=true, to_apply=%region_33.34 | all-reduce | flops 4112 | bytes 32896 | tf_op jit(solution)/shard_map/psum | solution.py:277
  1247.4 1187.8 %reduce-scatter.26.cloned.1.call-done = f32[128,16384]{1,0:T(8,128)} async-done(((f32[2048,16384]{1,0:T(8,128)}), f32[128,16384]{1,0:T(8,128)}) %reduce-scatter.26.cloned.1.call-update) | async-done | bytes 8388624 | tf_op jit(solution)/shard_map/reduce_scatter | solution.py:271
  (389 shorter events, 200.3 us)
Async XLA Ops:
  7.2 28.8 %all-gather.27.cloned.1.call-start = ((), (), s32[]{:S(2)}) async-start(), calls=%async_computation.17 | async-start | bytes 1572864 | tf_op jit(solution)/shard_map/all_gather | solution.py:20
  11.8 127.5 %all-gather.17.cloned.1.call-start = ((), (), s32[]{:S(2)}) async-start(), calls=%async_computation.10 | async-start | bytes 13369344 | tf_op jit(solution)/shard_map/all_gather | solution.py:243
  13.9 147.1 %all-gather.15.cloned.1.call-start = ((), (), s32[]{:S(2)}) async-start(), calls=%async_computation.9 | async-start | bytes 1572864 | tf_op jit(solution)/shard_map/all_gather | solution.py:20
  14.7 198.8 %all-gather.19.cloned.1.call-start = ((), (), s32[]{:S(2)}) async-start(), calls=%async_computation.11 | async-start | bytes 4456448 | tf_op jit(solution)/shard_map/all_gather | solution.py:244
  15.3 233.7 %reduce-scatter.14.cloned.1.call-start = ((), (), s32[]{:S(2)}) async-start(), calls=%async_computation.18 | async-start | bytes 3145728 | tf_op jit(solution)/shard_map/reduce_scatter | solution.py:24
  17.9 166.5 %copy-start.90 = (f32[128]{0:T(128)}, f32[128]{0:T(128)S(1)}, u32[]{:S(2)}) copy-start(f32[128]{0:T(128)S(1)} %get-tuple-element.171) | copy-start | bytes 1540
  17.9 167.2 %copy-start.88 = (f32[128]{0:T(128)}, f32[128]{0:T(128)S(1)}, u32[]{:S(2)}) copy-start(f32[128]{0:T(128)S(1)} %get-tuple-element.170) | copy-start | bytes 1540
  18.0 907.8 %copy-start.74 = (f32[8]{0:T(128)}, f32[8]{0:T(128)S(1)}, u32[]{:S(2)}) copy-start(f32[8]{0:T(128)S(1)} %get-tuple-element.108) | copy-start | bytes 100
  218.4 65.2 %reduce-scatter.10.cloned.1.call-start = ((), (), s32[]{:S(2)}) async-start(), calls=%async_computation.12 | async-start | bytes 3145728 | tf_op jit(solution)/shard_map/reduce_scatter | solution.py:24
  220.5 63.1 %copy-start.4 = (bf16[2,1,128,2048]{3,2,1,0:T(8,128)(2,1)S(1)}, bf16[2,1,128,2048]{3,2,1,0:T(8,128)(2,1)}, u32[]{:S(2)}) copy-start(bf16[2,1,128,2048]{3,2,1,0:T(8,128)(2,1)} %param.25) | copy-start | bytes 3145732
  225.5 60.1 %copy-start.58 = (f32[2048]{0:T(1024)S(1)}, f32[2048]{0:T(1024)}, u32[]{:S(2)}) copy-start(f32[2048]{0:T(1024)} %param.36) | copy-start | bytes 24580
  225.5 82.4 %all-gather.21.cloned.1.call-start = ((), (), s32[]{:S(2)}) async-start(), calls=%async_computation.13 | async-start | bytes 1572864 | tf_op jit(solution)/shard_map/all_gather | solution.py:20
  285.5 549.0 %copy-start = (f32[1,128,2048]{2,1,0:T(8,128)}, f32[1,128,2048]{2,1,0:T(8,128)S(1)}, u32[]{:S(2)}) copy-start(f32[1,128,2048]{2,1,0:T(8,128)S(1)} %get-tuple-element.146) | copy-start | bytes 3145732
  285.5 549.0 %copy-start.2 = (f32[1,128,2048]{2,1,0:T(8,128)}, f32[1,128,2048]{2,1,0:T(8,128)S(1)}, u32[]{:S(2)}) copy-start(f32[1,128,2048]{2,1,0:T(8,128)S(1)} %get-tuple-element.104) | copy-start | bytes 3145732
  285.5 549.0 %copy-start.72 = (f32[128]{0:T(128)}, f32[128]{0:T(128)S(1)}, u32[]{:S(2)}) copy-start(f32[128]{0:T(128)S(1)} %add_rsqrt_fusion.2) | copy-start | bytes 1540
  286.5 191.7 %all-gather.23.cloned.1.call-start = ((), (), s32[]{:S(2)}) async-start(), calls=%async_computation.14 | async-start | bytes 35651584 | tf_op jit(solution)/shard_map/all_gather | solution.py:245
  289.9 211.8 %all-gather.35.cloned.1.call-start = ((), (), s32[]{:S(2)}) async-start(), calls=%async_computation.28 | async-start | bytes 1572864 | tf_op jit(solution)/shard_map/all_gather | solution.py:20
  291.0 339.1 %all-gather.25.cloned.1.call-start = ((), (), s32[]{:S(2)}) async-start(), calls=%async_computation.15 | async-start | bytes 17825792 | tf_op jit(solution)/shard_map/all_gather | solution.py:246
  291.6 399.1 %reduce-scatter.18.cloned.1.call-start = ((), (), s32[]{:S(2)}) async-start(), calls=%async_computation.21 | async-start | bytes 3145728 | tf_op jit(solution)/shard_map/reduce_scatter | solution.py:24
  660.5 54.7 %all-gather.29.cloned.1.call-start = ((), (), s32[]{:S(2)}) async-start(), calls=%async_computation.19 | async-start | bytes 1572864 | tf_op jit(solution)/shard_map/all_gather | solution.py:20
  660.5 174.0 %copy-start.76 = (f32[128]{0:T(128)}, f32[128]{0:T(128)S(1)}, u32[]{:S(2)}) copy-start(f32[128]{0:T(128)S(1)} %add_rsqrt_fusion) | copy-start | bytes 1540
  693.7 44.3 %all-gather.37.cloned.1.call-start = ((), (), s32[]{:S(2)}) async-start(), calls=%async_computation.29 | async-start | bytes 1572864 | tf_op jit(solution)/shard_map/all_gather | solution.py:20
  694.4 106.0 %reduce-scatter.22.cloned.1.call-start = ((), (), s32[]{:S(2)}) async-start(), calls=%async_computation.24 | async-start | bytes 3145728 | tf_op jit(solution)/shard_map/reduce_scatter | solution.py:24
  768.4 66.1 %reduce-scatter.16.cloned.1.call-start = ((), (), s32[]{:S(2)}) async-start(), calls=%async_computation.20 | async-start | bytes 3145728 | tf_op jit(solution)/shard_map/reduce_scatter | solution.py:24
  781.1 53.5 %copy-start.6 = (f32[1,128,2048]{2,1,0:T(8,128)S(1)}, f32[1,128,2048]{2,1,0:T(8,128)}, u32[]{:S(2)}) copy-start(f32[1,128,2048]{2,1,0:T(8,128)} %reduce-scatter.18.cloned.1.call-done) | copy-start | bytes 3145732
  781.1 78.5 %all-gather.33.cloned.1.call-start = ((), (), s32[]{:S(2)}) async-start(), calls=%async_computation.25 | async-start | bytes 1572864 | tf_op jit(solution)/shard_map/all_gather | solution.py:20
  781.1 57.0 %copy-start.84 = (f32[128]{0:T(128)}, f32[128]{0:T(128)S(1)}, u32[]{:S(2)}) copy-start(f32[128]{0:T(128)S(1)} %broadcast_multiply_fusion.3) | copy-start | bytes 1540
  838.1 44.1 %all-gather.31.cloned.1.call-start = ((), (), s32[]{:S(2)}) async-start(), calls=%async_computation.22 | async-start | bytes 1572864 | tf_op jit(solution)/shard_map/all_gather | solution.py:20
  838.8 358.7 %reduce-scatter.24.cloned.1.call-start = ((), (), s32[]{:S(2)}) async-start(), calls=%async_computation.26 | async-start | bytes 3145728 | tf_op jit(solution)/shard_map/reduce_scatter | solution.py:24
  917.3 280.2 %reduce-scatter.20.cloned.1.call-start = ((), (), s32[]{:S(2)}) async-start(), calls=%async_computation.23 | async-start | bytes 3145728 | tf_op jit(solution)/shard_map/reduce_scatter | solution.py:24
  937.7 302.1 %reduce-scatter.12.cloned.1.call-start = ((), (), s32[]{:S(2)}) async-start(), calls=%async_computation.16 | async-start | bytes 3145728 | tf_op jit(solution)/shard_map/reduce_scatter | solution.py:24
  949.1 1486.1 %reduce-scatter.26.cloned.1.call-start = ((), (), s32[]{:S(2)}) async-start(), calls=%async_computation.27 | async-start | bytes 142606336 | tf_op jit(solution)/shard_map/reduce_scatter | solution.py:271
  (89 other events, 694.5 us)
Sparse Core Ops, SparseCore 0:
  11.9 24.0 all-gather.26
  38.8 100.4 all-gather.16
  141.4 19.5 all-gather.14
  163.0 50.3 all-gather.18
  218.5 30.4 reduce-scatter.13
  251.6 31.9 reduce-scatter.9
  286.7 21.2 all-gather.20
  310.1 168.0 all-gather.22
  480.3 21.2 all-gather.34
  503.6 126.4 all-gather.24
  660.6 30.0 reduce-scatter.17
  693.8 21.2 all-gather.28
  716.7 21.2 all-gather.36
  768.5 31.8 reduce-scatter.21
  802.6 31.8 reduce-scatter.15
  838.3 21.2 all-gather.32
  861.0 21.2 all-gather.30
  917.4 31.8 reduce-scatter.23
  951.6 31.9 reduce-scatter.19
  986.2 31.8 reduce-scatter.11
  1196.9 1238.2 reduce-scatter.25
where the time goes:
time: 2460 us; the launch traced here: 2450 us
  waiting for transfers between devices  1860 us (76%)
  matrix products  345 us (14%)
  other arithmetic  132 us (5%)
  local copies, waits for them, and re-layouts  55.9 us (2%)
  blocking collectives  39.8 us (2%)
    reduce_scatter x1, waiting for transfers between devices, on_device(): lax.psum_scatter(make_term([outcome[2] for outcome in outcomes]), 'dp', s...  1190 us
    all_gather x1, waiting for transfers between devices, on_device(): lax.all_gather(w_gu_part, 'dp', axis=0, tiled=True)  170 us
    dot_general x8, matrix products, make_term(): lax.dot_general(left_part, pairs[index][1], (((0,), (0,)), ((), ())), pre...  151 us
    reduce_scatter x8, waiting for transfers between devices, reduce_rows(): lax.psum_scatter(partial_value, 'mp', scatter_dimension=1, tiled=True)  139 us
    all_gather x1, waiting for transfers between devices, on_device(): lax.all_gather(w_down, 'dp', axis=0, tiled=True)  128 us
    all_gather x1, waiting for transfers between devices, on_device(): lax.all_gather(w_qkv_part, 'dp', axis=0, tiled=True)  103 us
    all_gather x8, waiting for transfers between devices, gather_rows(): return lax.all_gather(local_rows, 'mp', axis=1, tiled=True)  103 us
    dot_general x8, matrix products, fold_weights(): return jnp.dot(inputs, weight, preferred_element_type=jnp.float32)  86.2 us
  transfers between devices with their start and end apart: 21, of which 18 were waited for; matrix products, arithmetic and copies ran while one was open for 17% of the time, Pallas kernels for 0%

commit v1 on v0

--- a/solution.py
+++ b/solution.py
@@ -8,6 +8,18 @@
 masked_score = -1e30
 
 
+def doubled_up(x, axis, dim):
+    ways, here, step = (lax.axis_size(axis), lax.axis_index(axis), x.shape[dim])
+    line, have = (x, 1)
+    while have < ways:
+        line = jnp.concatenate(
+            [line, lax.ppermute(line, axis, [(d, (d - have) % ways) for d in range(ways)])],
+            axis=dim,
+        )
+        have = 2 * have
+    return jnp.roll(line, here * step, axis=dim)
+
+
 def positive_map(values):
     return jnp.where(values > 0.0, values + 1.0, jnp.exp(jnp.minimum(values, 0.0)))
 
@@ -17,7 +29,7 @@
 
 
 def gather_rows(local_rows):
-    return lax.all_gather(local_rows, "mp", axis=1, tiled=True)
+    return doubled_up(local_rows, "mp", 1)
 
 
 def reduce_rows(partial_value):

time: 2460 us -> 2350 us (0.955)
  waiting for transfers between devices: 1860 us -> 1710 us
    all_gather x8 -> x0, waiting for transfers between devices: 103 us -> none  [gather_rows(): return lax.all_gather(local_rows, 'mp', axis=1, tiled=True)]
    ppermute x0 -> x8, waiting for transfers between devices: none -> 37.8 us  [doubled_up(): lax.ppermute(line, axis, [(d, (d - have) % ways) for d in range(ways)])]
    all_gather x1, waiting for transfers between devices: 103 us -> 74.4 us  [on_device(): lax.all_gather(w_qkv_part, 'dp', axis=0, tiled=True)]
  transfers between devices with their start and end apart: 21 -> 21, of which waited for: 18 -> 13; matrix products, arithmetic and copies ran while one was open for 17% -> 17% of each run, Pallas kernels for 0% -> 0%
where the time goes in v1:
time: 2350 us; the launch traced here: 2330 us
  waiting for transfers between devices  1710 us (73%)
  matrix products  340 us (14%)
  other arithmetic  146 us (6%)
  local copies, waits for them, and re-layouts  76.3 us (3%)
  blocking collectives  40 us (2%)
    reduce_scatter x1, waiting for transfers between devices, on_device(): lax.psum_scatter(make_term([outcome[2] for outcome in outcomes]), 'dp', s...  1190 us
    all_gather x1, waiting for transfers between devices, on_device(): lax.all_gather(w_gu_part, 'dp', axis=0, tiled=True)  152 us
    reduce_scatter x8, waiting for transfers between devices, reduce_rows(): lax.psum_scatter(partial_value, 'mp', scatter_dimension=1, tiled=True)  143 us
    dot_general x8, matrix products, make_term(): lax.dot_general(left_part, pairs[index][1], (((0,), (0,)), ((), ())), pre...  140 us
    all_gather x1, waiting for transfers between devices, on_device(): lax.all_gather(w_down, 'dp', axis=0, tiled=True)  110 us
    dot_general x8, matrix products, fold_weights(): return jnp.dot(inputs, weight, preferred_element_type=jnp.float32)  88.4 us
    concatenate x1, other arithmetic, make_term(): return jnp.concatenate(columns, axis=1)  86.1 us
    dot_general x8, matrix products, map_weights(): lax.dot_general(inputs, weight, (((1,), (1,)), ((), ())), preferred_eleme...  85.6 us
  transfers between devices with their start and end apart: 21, of which 13 were waited for; matrix products, arithmetic and copies ran while one was open for 17% of the time, Pallas kernels for 0%

profile of v1, /device:TPU:0, one launch (start us, length us, event | category | flops | bytes accessed | tf_op | source)
XLA Modules:
  0.0 2334.9 jit_solution(7170223940809669042)
XLA Ops:
  18.2 8.6 collective-permute-done
  29.2 8.0 collective-permute-done.2
  39.6 74.4 %all-gather.5.cloned.1.call-done = bf16[2048,3072]{1,0:T(8,128)(2,1)} async-done(((bf16[128,3072]{1,0:T(8,128)(2,1)}), bf16[2048,3072]{1,0:T(8,128)(2,1)}) %all-gather.5.cloned.1.call-update) | async-done | bytes 12582928 | tf_op jit(solution)/shard_map/all_gather | solution.py:255
  114.1 8.0 convolution_convert_fusion
  129.7 8.0 convolution_convert_fusion.1
  184.7 27.4 %reduce-scatter.14.cloned.1.call-done = f32[1,128,2048]{2,1,0:T(8,128)} async-done(((f32[1,256,2048]{2,1,0:T(8,128)}), f32[1,128,2048]{2,1,0:T(8,128)}) %reduce-scatter.14.cloned.1.call-update) | async-done | bytes 1048592 | tf_op jit(solution)/shard_map/reduce_scatter | solution.py:36
  212.1 34.6 %reduce-scatter.10.cloned.1.call-done = f32[1,128,2048]{2,1,0:T(8,128)} async-done(((f32[1,256,2048]{2,1,0:T(8,128)}), f32[1,128,2048]{2,1,0:T(8,128)}) %reduce-scatter.10.cloned.1.call-update) | async-done | bytes 1048592 | tf_op jit(solution)/shard_map/reduce_scatter | solution.py:36
  251.7 10.6 collective-permute-done.1
  265.1 151.7 %all-gather.9.cloned.1.call-done = bf16[2048,8192]{1,0:T(8,128)(2,1)} async-done(((bf16[128,8192]{1,0:T(8,128)(2,1)}), bf16[2048,8192]{1,0:T(8,128)(2,1)}) %all-gather.9.cloned.1.call-update) | async-done | bytes 33554448 | tf_op jit(solution)/shard_map/all_gather | solution.py:257
  416.7 18.8 fusion.202
  435.6 109.6 %all-gather.11.cloned.1.call-done = bf16[2048,4096]{1,0:T(8,128)(2,1)} async-done(((bf16[128,4096]{1,0:T(8,128)(2,1)}), bf16[2048,4096]{1,0:T(8,128)(2,1)}) %all-gather.11.cloned.1.call-update) | async-done | bytes 16777232 | tf_op jit(solution)/shard_map/all_gather | solution.py:258
  545.2 15.7 multiply_convert_fusion.3
  560.9 17.2 convolution_bitcast_fusion.3
  580.6 36.6 %reduce-scatter.18.cloned.1.call-done = f32[1,128,2048]{2,1,0:T(8,128)} async-done(((f32[1,256,2048]{2,1,0:T(8,128)}), f32[1,128,2048]{2,1,0:T(8,128)}) %reduce-scatter.18.cloned.1.call-update) | async-done | bytes 1048592 | tf_op jit(solution)/shard_map/reduce_scatter | solution.py:36
  622.6 10.6 collective-permute-done.3
  635.0 17.5 fusion.203
  652.4 15.7 multiply_convert_fusion.1
  668.2 17.2 convolution_bitcast_fusion.1
  685.7 13.0 convolution_bitcast_fusion.4
  703.0 12.6 reduce-scatter.22.cloned.1.call-done
  717.7 32.1 %reduce-scatter.16.cloned.1.call-done = f32[1,128,2048]{2,1,0:T(8,128)} async-done(((f32[1,256,2048]{2,1,0:T(8,128)}), f32[1,128,2048]{2,1,0:T(8,128)}) %reduce-scatter.16.cloned.1.call-update) | async-done | bytes 1048592 | tf_op jit(solution)/shard_map/reduce_scatter | solution.py:36
  753.8 13.7 fusion.205
  845.7 12.4 convolution_bitcast_fusion.5
  858.1 25.6 %fusion.2 = f32[2048,8192]{1,0:T(8,128)} fusion(bf16[256,2048]{1,0:T(8,128)(2,1)S(1)} %copy-done.28, bf16[256,4096]{1,0:T(8,128)(2,1)} %get-tuple-element.111, bf16[256,4096]{1,0:T(8,128)(2,1)} %get-tuple-element.110), kind=kOutput, calls=%fused_computation.27 | convolution fusion | flops 8598323200 | bytes 72351744 | tf_op jit(solution)/shard_map/dot_general | solution.py:55
  884.9 22.3 convolution_add_fusion.1
  907.2 44.1 %convolution_add_fusion = f32[2048,8192]{1,0:T(8,128)} fusion(f32[2048,8192]{1,0:T(8,128)} %fusion.2, bf16[256,2048]{1,0:T(8,128)(2,1)S(1)} %copy-done.32, bf16[256,4096]{1,0:T(8,128)(2,1)} %get-tuple-element.113, bf16[256,4096]{1,0:T(8,128)(2,1)} %get-tuple-element.112), kind=kOutput, calls=%fused_computation.3 | convolution fusion | flops 8615100416 | bytes 139460608 | tf_op jit(solution)/shard_map/dot_general | solution.py:55
  951.2 11.7 fusion.204
  969.1 9.4 copy.136
  978.5 16.5 convolution_add_fusion.2
  995.0 86.1 %pad_maximum_fusion = f32[2048,16384]{1,0:T(8,128)} fusion(f32[2048,4096]{1,0:T(8,128)} %convolution_add_fusion.1, f32[2048,8192]{1,0:T(8,128)} %convolution_add_fusion, f32[2048,1024]{1,0:T(8,128)} %copy.136, f32[2048,3072]{1,0:T(8,128)} %convolution_add_fusion.2), kind=kLoop, calls=%fused_computation.2 | loop fusion | flops 100663296 | bytes 268435456 | tf_op jit(solution)/shard_map/concatenate | solution.py:63
  1084.5 40.0 %all-reduce = (f32[2048]{0:T(1024)}, f32[2048]{0:T(1024)}, f32[16]{0:T(128)}) all-reduce(f32[2048]{0:T(1024)S(1)} %add.332, f32[2048]{0:T(1024)S(1)} %add.333, f32[16]{0:T(128)S(1)} %fusion.176), channel_id=1, replica_groups=mesh['dp'=16,'mp'=2] {'dp','mp'}, use_global_device_ids=true, to_apply=%region_33.35 | all-reduce | flops 4112 | bytes 32896 | tf_op jit(solution)/shard_map/psum | solution.py:289
  1132.2 1187.1 %reduce-scatter.26.cloned.1.call-done = f32[128,16384]{1,0:T(8,128)} async-done(((f32[2048,16384]{1,0:T(8,128)}), f32[128,16384]{1,0:T(8,128)}) %reduce-scatter.26.cloned.1.call-update) | async-done | bytes 8388624 | tf_op jit(solution)/shard_map/reduce_scatter | solution.py:283
  (453 shorter events, 202.2 us)
Async XLA Ops:
  7.2 106.9 %all-gather.5.cloned.1.call-start = ((), (), s32[]{:S(2)}) async-start(), calls=%async_computation.9 | async-start | bytes 13369344 | tf_op jit(solution)/shard_map/all_gather | solution.py:255
  9.4 156.1 %all-gather.7.cloned.1.call-start = ((), (), s32[]{:S(2)}) async-start(), calls=%async_computation.10 | async-start | bytes 4456448 | tf_op jit(solution)/shard_map/all_gather | solution.py:256
  10.1 201.9 %reduce-scatter.14.cloned.1.call-start = ((), (), s32[]{:S(2)}) async-start(), calls=%async_computation.15 | async-start | bytes 3145728 | tf_op jit(solution)/shard_map/reduce_scatter | solution.py:36
  10.9 15.9 collective-permute-start
  13.9 23.3 collective-permute-start.2
  17.9 141.2 %copy-start.122 = (f32[128]{0:T(128)}, f32[128]{0:T(128)S(1)}, u32[]{:S(2)}) copy-start(f32[128]{0:T(128)S(1)} %get-tuple-element.172) | copy-start | bytes 1540
  17.9 143.0 %copy-start.120 = (f32[128]{0:T(128)}, f32[128]{0:T(128)S(1)}, u32[]{:S(2)}) copy-start(f32[128]{0:T(128)S(1)} %get-tuple-element.171) | copy-start | bytes 1540
  18.0 145.0 %copy-start.105 = (f32[8]{0:T(128)}, f32[8]{0:T(128)S(1)}, u32[]{:S(2)}) copy-start(f32[8]{0:T(128)S(1)} %get-tuple-element.109) | copy-start | bytes 100
  29.2 100.5 %copy-start.18 = (bf16[256,2048]{1,0:T(8,128)(2,1)}, bf16[256,2048]{1,0:T(8,128)(2,1)S(1)}, u32[]{:S(2)}) copy-start(bf16[256,2048]{1,0:T(8,128)(2,1)S(1)} %fusion.97) | copy-start | bytes 3145732
  39.6 82.4 %copy-start.12 = (bf16[256,2048]{1,0:T(8,128)(2,1)}, bf16[256,2048]{1,0:T(8,128)(2,1)S(1)}, u32[]{:S(2)}) copy-start(bf16[256,2048]{1,0:T(8,128)(2,1)S(1)} %fusion.89) | copy-start | bytes 3145732
  170.4 76.2 %reduce-scatter.10.cloned.1.call-start = ((), (), s32[]{:S(2)}) async-start(), calls=%async_computation.11 | async-start | bytes 3145728 | tf_op jit(solution)/shard_map/reduce_scatter | solution.py:36
  178.3 238.4 %all-gather.9.cloned.1.call-start = ((), (), s32[]{:S(2)}) async-start(), calls=%async_computation.12 | async-start | bytes 35651584 | tf_op jit(solution)/shard_map/all_gather | solution.py:257
  181.3 363.9 %all-gather.11.cloned.1.call-start = ((), (), s32[]{:S(2)}) async-start(), calls=%async_computation.13 | async-start | bytes 17825792 | tf_op jit(solution)/shard_map/all_gather | solution.py:258
  181.9 435.3 %reduce-scatter.18.cloned.1.call-start = ((), (), s32[]{:S(2)}) async-start(), calls=%async_computation.17 | async-start | bytes 3145728 | tf_op jit(solution)/shard_map/reduce_scatter | solution.py:36
  183.6 65.0 %copy-start.82 = (f32[2048]{0:T(1024)S(1)}, f32[2048]{0:T(1024)}, u32[]{:S(2)}) copy-start(f32[2048]{0:T(1024)} %param.38) | copy-start | bytes 24580
  183.6 65.6 %collective-permute-start.4 = (bf16[1,128,2048]{2,1,0:T(8,128)(2,1)}, bf16[1,128,2048]{2,1,0:T(8,128)(2,1)}, u32[]{:S(2)}, u32[]{:S(2)}) collective-permute-start(bf16[1,128,2048]{2,1,0:T(8,128)(2,1)} %get-tuple-element.142), channel_id=1, source_target_pairs={{0,1},{1,0},{2,3},{3,2},{4,5},{5,4},{6,7},{7,6},{8,9},{9,8},{10,11... | collective-permute-start | bytes 1572872 | tf_op jit(solution)/shard_map/ppermute | solution.py:16
  248.5 501.3 %copy-start = (f32[1,128,2048]{2,1,0:T(8,128)}, f32[1,128,2048]{2,1,0:T(8,128)S(1)}, u32[]{:S(2)}) copy-start(f32[1,128,2048]{2,1,0:T(8,128)S(1)} %get-tuple-element.147) | copy-start | bytes 3145732
  248.5 501.3 %copy-start.2 = (f32[1,128,2048]{2,1,0:T(8,128)}, f32[1,128,2048]{2,1,0:T(8,128)S(1)}, u32[]{:S(2)}) copy-start(f32[1,128,2048]{2,1,0:T(8,128)S(1)} %get-tuple-element.105) | copy-start | bytes 3145732
  248.6 501.3 %copy-start.103 = (f32[128]{0:T(128)}, f32[128]{0:T(128)S(1)}, u32[]{:S(2)}) copy-start(f32[128]{0:T(128)S(1)} %add_rsqrt_fusion.2) | copy-start | bytes 1540
  248.7 13.6 collective-permute-start.1
  251.7 293.5 %copy-start.16 = (bf16[256,2048]{1,0:T(8,128)(2,1)}, bf16[256,2048]{1,0:T(8,128)(2,1)S(1)}, u32[]{:S(2)}) copy-start(bf16[256,2048]{1,0:T(8,128)(2,1)S(1)} %fusion.81) | copy-start | bytes 3145732
  578.1 137.5 %reduce-scatter.22.cloned.1.call-start = ((), (), s32[]{:S(2)}) async-start(), calls=%async_computation.19 | async-start | bytes 3145728 | tf_op jit(solution)/shard_map/reduce_scatter | solution.py:36
  579.2 41.7 %collective-permute-start.6 = (bf16[1,128,2048]{2,1,0:T(8,128)(2,1)S(1)}, bf16[1,128,2048]{2,1,0:T(8,128)(2,1)S(1)}, u32[]{:S(2)}, u32[]{:S(2)}) collective-permute-start(bf16[1,128,2048]{2,1,0:T(8,128)(2,1)S(1)} %copy-done.67), channel_id=1, source_target_pairs={{0,1},{1,0},{2,3},{3,2},{4,5},{5,4},{6,7},{7,6},{8,9},{9,8},{10,11... | collective-permute-start | bytes 1572872 | tf_op jit(solution)/shard_map/ppermute | solution.py:16
  580.6 169.2 %copy-start.108 = (f32[128]{0:T(128)}, f32[128]{0:T(128)S(1)}, u32[]{:S(2)}) copy-start(f32[128]{0:T(128)S(1)} %add_rsqrt_fusion) | copy-start | bytes 1540
  619.4 13.8 collective-permute-start.3
  685.4 64.4 %reduce-scatter.16.cloned.1.call-start = ((), (), s32[]{:S(2)}) async-start(), calls=%async_computation.16 | async-start | bytes 3145728 | tf_op jit(solution)/shard_map/reduce_scatter | solution.py:36
  698.6 383.3 %reduce-scatter.24.cloned.1.call-start = ((), (), s32[]{:S(2)}) async-start(), calls=%async_computation.20 | async-start | bytes 3145728 | tf_op jit(solution)/shard_map/reduce_scatter | solution.py:36
  753.4 15.8 collective-permute-start.7
  767.5 15.6 collective-permute-start.5
  820.6 261.3 %reduce-scatter.20.cloned.1.call-start = ((), (), s32[]{:S(2)}) async-start(), calls=%async_computation.18 | async-start | bytes 3145728 | tf_op jit(solution)/shard_map/reduce_scatter | solution.py:36
  845.6 278.8 %reduce-scatter.12.cloned.1.call-start = ((), (), s32[]{:S(2)}) async-start(), calls=%async_computation.14 | async-start | bytes 3145728 | tf_op jit(solution)/shard_map/reduce_scatter | solution.py:36
  883.7 1435.6 %reduce-scatter.26.cloned.1.call-start = ((), (), s32[]{:S(2)}) async-start(), calls=%async_computation.21 | async-start | bytes 142606336 | tf_op jit(solution)/shard_map/reduce_scatter | solution.py:283
  (121 other events, 838.0 us)
Sparse Core Ops, SparseCore 0:
  10.9 103.1 all-gather.4
  116.2 48.6 all-gather.6
  170.5 41.4 reduce-scatter.13
  214.7 31.8 reduce-scatter.9
  248.7 168.0 all-gather.8
  418.8 126.4 all-gather.10
  578.3 38.9 reduce-scatter.17
  685.5 30.0 reduce-scatter.21
  717.9 31.9 reduce-scatter.15
  820.7 31.8 reduce-scatter.23
  854.9 31.8 reduce-scatter.19
  888.9 31.8 reduce-scatter.11
  1081.3 1238.0 reduce-scatter.25
